TPU v7x, 32 devices: a whole 2x2x4 slice. The times are simulated.
32 devices in a mesh: dp: 4 (over z), lat: 4 (over y, core), lon: 2 (over x).
Axes of the slice: x: 2, y: 2, z: 4, core: 2. Of those that a mesh axis runs over, the one named last changes fastest.
Arguments:
- projected: bfloat16 [4, 4, 32, 16, 4608], P('dp', None, 'lat', 'lon'), may hold values from -52 to 52
- targets: bfloat16 [4, 4, 32, 16, 160], P('dp', None, 'lat', 'lon'), may hold values from -6 to 6
- valid_cells: int32 [32, 16], P('lat', 'lon'), may hold values 0 or 1
- w_out: bfloat16 [1536, 1536], P('dp'), may hold values from -0.15625 to 0.15625
- unpatch_matrix: bfloat16 [1536, 160], P('dp'), may hold values from -0.15625 to 0.15625
- norm_gain: bfloat16 [1536], P('dp'), may hold values from 0.099609375 to 1.8984375
- var_weight: float32 [5], replicated, may hold values from 0.3 to 3
Outputs:
- grad_context: bfloat16 [4, 4, 32, 16, 1536], P('dp', None, 'lat', 'lon')
- grad_recovery: float32 [1536, 160], P('dp')
- sample_penalty: float32 [4], P('dp')
All inputs are finite; a program needn't handle non-finite values. No bound on the sum of `valid_cells` on one device may be relied on, other than what follows from the above.
Results may differ from a plain program's by a relative error of at most 0.011.
Values may be sent and summed in bfloat16 or wider, within the bound.
No kernel may reach another device: no remote copies, remote signals or barrier semaphores. Data moves between devices by JAX's collectives and lax.ppermute only.
A program may use at most 64 MiB of HBM per device.

v0:
```python
import math
import jax
import jax.numpy as jnp
from jax import lax
from jax.sharding import PartitionSpec as P

HEADS = 48
HDIM = 32
WLEV = 2


def from_behind(array, axis, by):
    length = lax.axis_size(axis)
    return lax.ppermute(array, axis, [(i, (i + by) % length) for i in range(length)])


def shards(projected, targets, valid_cells, w_out, unpatch_matrix, norm_gain, var_weight):
    tile_side = projected.shape[2]
    half_side = tile_side // 2
    levels = projected.shape[1]
    model_width = w_out.shape[1]
    predicted_span = unpatch_matrix.shape[1]
    lat_total = tile_side * lax.axis_size("lat")
    lon_total = tile_side * lax.axis_size("lon")
    lat_place = lax.axis_index("lat")
    moved = from_behind(
        (projected[:, :, :, :half_side], targets[:, :, :, :half_side], valid_cells[:, :half_side]),
        "lon",
        -1,
    )
    strip_proj = jnp.concatenate([projected[:, :, :, half_side:], moved[0]], axis=3)
    strip_goal = jnp.concatenate([targets[:, :, :, half_side:], moved[1]], axis=3)
    strip_valid = jnp.concatenate([valid_cells[:, half_side:], moved[2]], axis=1)
    moved_rows = from_behind(
        (strip_proj[:, :, :half_side], strip_goal[:, :, :half_side], strip_valid[:half_side]),
        "lat",
        -1,
    )
    local_proj = jnp.concatenate([strip_proj[:, :, half_side:], moved_rows[0]], axis=2)
    shard_reference = jnp.concatenate([strip_goal[:, :, half_side:], moved_rows[1]], axis=2)
    local_valid = jnp.concatenate([strip_valid[half_side:], moved_rows[2]], axis=0).astype(
        jnp.float32
    )
    win_count = levels // WLEV
    tokw = WLEV * tile_side * tile_side
    windows = local_proj.reshape(win_count, tokw, 3 * model_width)
    rows_here = lat_place * tile_side + jnp.arange(tile_side)
    region_rows = (rows_here >= lat_total - half_side).astype(jnp.int32)
    region = jnp.broadcast_to(region_rows[None, :, None], (WLEV, tile_side, tile_side)).reshape(-1)
    allowed = region[:, None] == region[None, :]
    queries = windows[..., :model_width].reshape(win_count, tokw, HEADS, -1)
    key_heads = windows[..., model_width : 2 * model_width].reshape(win_count, tokw, HEADS, -1)
    value_heads = windows[..., 2 * model_width :].reshape(win_count, tokw, HEADS, -1)
    scores = jnp.einsum("wqhd,wkhd->whqk", queries, key_heads, preferred_element_type=jnp.float32)
    scores = scores * (1.0 / math.sqrt(HDIM))
    scores = jnp.where(allowed[None, None], scores, -1e30)
    row_peak = jnp.max(scores, axis=-1, keepdims=True)
    lifted = jnp.exp(scores - row_peak)
    attn = (lifted / jnp.sum(lifted, axis=-1, keepdims=True)).astype(jnp.bfloat16)
    context = jnp.einsum("whqk,wkhd->wqhd", attn, value_heads, preferred_element_type=jnp.float32)
    context = context.astype(jnp.bfloat16).reshape(win_count * tokw, model_width)
    element_total = win_count * tokw
    out_all, unprojected_pieces, gain_all = (
        lax.all_gather(w_out, "dp", axis=0, tiled=True),
        lax.all_gather(unpatch_matrix, "dp", axis=0, tiled=True),
        lax.all_gather(norm_gain, "dp", axis=0, tiled=True),
    )
    mixed_rows = jnp.dot(context, out_all, preferred_element_type=jnp.float32)
    centre = jnp.mean(mixed_rows, axis=-1, keepdims=True)
    spread = jnp.mean((mixed_rows - centre) ** 2, axis=-1, keepdims=True)
    inv_spread = lax.rsqrt(spread + 1e-05)
    normed = (mixed_rows - centre) * inv_spread
    gain_f = gain_all.astype(jnp.float32)
    latent_activation = (normed * gain_f).astype(jnp.bfloat16)
    prediction_field = jnp.dot(
        latent_activation, unprojected_pieces, preferred_element_type=jnp.float32
    )
    prediction_misfit = prediction_field - shard_reference.reshape(
        element_total, predicted_span
    ).astype(jnp.float32)
    all_rows = jnp.arange(lat_total).astype(jnp.float32)
    cosine_mean = jnp.mean(jnp.cos(math.pi * ((all_rows + 0.5) / lat_total - 0.5)))
    initial_rows = ((rows_here + half_side) % lat_total).astype(jnp.float32)
    lat_here = jnp.cos(math.pi * ((initial_rows + 0.5) / lat_total - 0.5)) / cosine_mean
    element_factor = jnp.broadcast_to(
        lat_here[None, :, None] * local_valid[None], (levels, tile_side, tile_side)
    ).reshape(element_total, 1)
    variable_factor = jnp.repeat(var_weight, predicted_span // var_weight.shape[0])[None, :]
    shard_penalty = jnp.sum(
        element_factor * variable_factor * prediction_misfit * prediction_misfit
    ) / (levels * lat_total * lon_total * (predicted_span // var_weight.shape[0]))
    prediction_gradient = (2.0 * element_factor * variable_factor * prediction_misfit).astype(
        jnp.bfloat16
    )
    grad_shard = lax.psum_scatter(
        jnp.einsum(
            "td,to->do", latent_activation, prediction_gradient, preferred_element_type=jnp.float32
        ).astype(jnp.bfloat16),
        "dp",
        scatter_dimension=0,
        tiled=True,
    ).astype(jnp.float32)
    grad_sum, loss_sum = lax.psum((grad_shard, shard_penalty), ("lat", "lon"))
    grad_recovery = grad_sum / (levels * lat_total * lon_total)
    grad_hidden = jnp.einsum(
        "to,do->td", prediction_gradient, unprojected_pieces, preferred_element_type=jnp.float32
    )
    scaled_grad = grad_hidden * gain_f
    grad_mixed = inv_spread * (
        scaled_grad
        - jnp.mean(scaled_grad, axis=-1, keepdims=True)
        - normed * jnp.mean(scaled_grad * normed, axis=-1, keepdims=True)
    )
    grad_mixed = grad_mixed.astype(jnp.bfloat16)
    grad_context = jnp.einsum("tj,ij->ti", grad_mixed, out_all, preferred_element_type=jnp.float32)
    grad_context = grad_context.astype(jnp.bfloat16).reshape(
        1, levels, tile_side, tile_side, model_width
    )
    return (grad_context, grad_recovery, loss_sum.reshape(1))


def solution(mesh):
    placed = (
        P("dp", None, "lat", "lon", None),
        P("dp", None, "lat", "lon", None),
        P("lat", "lon"),
        P("dp", None),
        P("dp", None),
        P("dp"),
        P(),
    )
    return jax.shard_map(
        shards,
        mesh=mesh,
        in_specs=placed,
        out_specs=(P("dp", None, "lat", "lon", None), P("dp", None), P("dp")),
        check_vma=False,
    )
```

profile of v0, /device:TPU:0, one launch (start us, length us, event | category | flops | bytes accessed | tf_op | source)
XLA Modules:
  0.0 177.8 jit_solution(18439652945624654499)
XLA Ops:
  7.2 0.7 all-gather.3.cloned.1.call-update
  7.9 3.3 %fusion.33 = (bf16[1,4,8,4,4608]{4,3,2,1,0:T(4,128)(2,1)S(1)}, bf16[1,4,8,4,4608]{4,3,2,1,0:T(4,128)(2,1)S(1)}) fusion(bf16[1,4,8,8,4608]{4,3,2,1,0:T(8,128)(2,1)} %param.7), kind=kLoop, calls=%fused_computation.70 | loop fusion | bytes 4718592 | tf_op jit(solution)/shard_map/slice | solution.py:31
  11.5 3.0 %collective-permute-start = (bf16[1,4,8,4,4608]{4,2,3,1,0:T(8,128)(2,1)S(1)}, bf16[1,4,8,4,4608]{4,2,3,1,0:T(8,128)(2,1)}, u32[]{:S(2)}, u32[]{:S(2)}) collective-permute-start(bf16[1,4,8,4,4608]{4,2,3,1,0:T(8,128)(2,1)S(1)} %copy.37), channel_id=1, source_target_pairs={{0,1},{1,0},{2,3},{3,2},{4,5},{5,4},{6,7},{7,6},{8,9},{9,8},{10,11... | collective-permute-start | bytes 3538952 | tf_op jit(solution)/shard_map/ppermute | solution.py:14
  14.5 0.6 fusion.36
  15.5 1.7 collective-permute-start.4
  17.4 13.0 %all-gather = bf16[4,1,384]{2,1,0:T(2,128)(2,1)S(1)} all-gather(bf16[1,1,384]{2,1,0:T(2,128)(2,1)S(1)} %reshape.165), channel_id=1, replica_groups=mesh['dp'=4,'lat'=4,'lon'=2] {'dp'}, dimensions={0}, use_global_device_ids=true | all-gather | bytes 3840 | tf_op jit(solution)/shard_map/all_gather | solution.py:66
  30.4 0.6 cosine_reduce_fusion
  31.7 0.6 fusion.27
  32.3 21.7 %all_gather.11 = bf16[1536,160]{0,1:T(8,128)(2,1)S(1)} all-gather(bf16[384,160]{0,1:T(8,128)(2,1)S(1)} %copy-done.4), channel_id=1, replica_groups=mesh['dp'=4,'lat'=4,'lon'=2] {'dp'}, dimensions={0}, use_global_device_ids=true | all-gather | bytes 614400 | tf_op jit(solution)/shard_map/all_gather | solution.py:65
  54.0 0.7 broadcast_compare_fusion
  54.7 1.9 %copy.27 = bf16[1,4,8,4,4608]{4,3,2,1,0:T(4,128)(2,1)S(1)} copy(bf16[1,4,8,4,4608]{4,2,3,1,0:T(8,128)(2,1)} %collective-permute-done) | data formatting | bytes 2359296 | tf_op jit(solution)/shard_map/ppermute | solution.py:14
  56.6 2.2 %fusion.8 = (bf16[1,4,4,8,4608]{4,3,2,1,0:T(8,128)(2,1)S(1)}, bf16[1,4,4,8,4608]{4,3,2,1,0:T(8,128)(2,1)}) fusion(bf16[1,4,8,4,4608]{4,3,2,1,0:T(4,128)(2,1)S(1)} %get-tuple-element.12, bf16[1,4,8,4,4608]{4,3,2,1,0:T(4,128)(2,1)S(1)} %copy.27), kind=kLoop, calls=%fused_computation.22 | loop fusion | flops 4718592 | bytes 4718592 | tf_op jit(solution)/shard_map/concatenate | solution.py:31
  58.9 1.6 collective-permute-start.3
  60.6 12.2 %collective-permute-done.3 = s32[4,8]{1,0:T(4,128)S(1)} collective-permute-done((s32[4,8]{1,0:T(4,128)S(1)}, s32[4,8]{1,0:T(4,128)S(1)}, u32[]{:S(2)}, u32[]{:S(2)}) %collective-permute-start.3) | collective-permute-done | bytes 160 | tf_op jit(solution)/shard_map/ppermute | solution.py:14
  73.1 2.5 %collective-permute-start.5 = (bf16[1,4,4,8,160]{4,3,2,1,0:T(8,128)(2,1)S(1)}, bf16[1,4,4,8,160]{4,3,2,1,0:T(8,128)(2,1)S(1)}, u32[]{:S(2)}, u32[]{:S(2)}) collective-permute-start(bf16[1,4,4,8,160]{4,3,2,1,0:T(8,128)(2,1)S(1)} %get-tuple-element.17), channel_id=1, source_target_pairs={{0,6},{2,0},{4,2},{6,4},{1,7},{3,1},{5,3},{7,5},{8,14},{10,8},{12,... | collective-permute-start | bytes 122888 | tf_op jit(solution)/shard_map/ppermute | solution.py:14
  75.5 1.9 %collective-permute-done.5 = bf16[1,4,4,8,160]{4,3,2,1,0:T(8,128)(2,1)S(1)} collective-permute-done((bf16[1,4,4,8,160]{4,3,2,1,0:T(8,128)(2,1)S(1)}, bf16[1,4,4,8,160]{4,3,2,1,0:T(8,128)(2,1)S(1)}, u32[]{:S(2)}, u32[]{:S(2)}) %collective-permute-start.5) | collective-permute-done | bytes 40992 | tf_op jit(solution)/shard_map/ppermute | solution.py:14
  78.1 1.2 copy.29
  79.2 1.2 copy.30
  80.4 1.2 copy.28
  81.6 4.2 %fusion.37 = (f32[2,48,128]{2,1,0:T(8,128)S(1)}, f32[2,48,128,128]{2,3,1,0:T(8,128)}) fusion(pred[128,128]{0,1:T(8,128)(4,1)S(1)} %copy-done.5, bf16[2,128,48,32]{1,3,2,0:T(8,128)(2,1)S(1)} %bitcast.35, bf16[2,128,48,32]{1,3,2,0:T(8,128)(2,1)S(1)} %bitcast.36), kind=kOutput, calls=%fused_computation.74 | convolution fusion | flops 106954880 | bytes 7929856 | tf_op jit(solution)/shard_map/sub | solution.py:58
  85.7 3.7 %fusion.7 = bf16[2,128,48,32]{1,3,2,0:T(8,128)(2,1)S(1)} fusion(bf16[2,128,48,32]{1,3,2,0:T(8,128)(2,1)S(1)} %bitcast.37, f32[2,48,128,128]{2,3,1,0:T(8,128)} %get-tuple-element.25, f32[2,48,128]{2,1,0:T(8,128)S(1)} %get-tuple-element.24), kind=kOutput, calls=%fused_computation.21 | convolution fusion | flops 104202240 | bytes 7913472 | tf_op jit(solution)/shard_map/whqk,wkhd->wqhd/dot_general | solution.py:60
  89.5 0.8 copy.32
  90.3 19.3 %all-gather.3.cloned.1.call-done = bf16[1536,1536]{1,0:T(8,128)(2,1)} async-done(((bf16[384,1536]{1,0:T(8,128)(2,1)}), bf16[1536,1536]{1,0:T(8,128)(2,1)}) %all-gather.3.cloned.1.call-update) | async-done | bytes 4718608 | tf_op jit(solution)/shard_map/all_gather | solution.py:64
  109.6 3.8 %fusion.38 = (f32[256]{0:T(256)S(1)}, f32[256,1536]{1,0:T(8,128)S(1)}) fusion(bf16[1536,1536]{1,0:T(8,128)(2,1)} %all-gather.3.cloned.1.call-done, bf16[192,8,2,128]{3,2,1,0:T(2,128)(2,1)S(1)} %bitcast.38), kind=kOutput, calls=%fused_computation.75 | convolution fusion | flops 1208352512 | bytes 7078912 | tf_op jit(solution)/shard_map/dot_general | solution.py:68
  114.4 0.7 fusion.18
  115.5 1.2 copy.35
  117.3 0.6 fusion.31
  117.9 4.8 %convolution_convert_fusion = bf16[256,1536]{1,0:T(8,128)(2,1)} fusion(bf16[1536,1536]{1,0:T(8,128)(2,1)} %all-gather.3.cloned.1.call-done, f32[256,1536]{1,0:T(8,128)S(1)} %get-tuple-element.28, f32[256,1536]{1,0:T(8,128)S(1)} %get-tuple-element.27, f32[256]{0:T(256)S(1)} %get-tuple-element.29, f32[256]{0:T(256)S(1)} %get-tuple-element.30, ...), kind=kOutput, calls=%fused_computation.10 | convolution fusion | flops 1211105280 | bytes 8654848 | tf_op jit(solution)/shard_map/tj,ij->ti/dot_general | solution.py:115
  122.7 15.9 %reduce-scatter.4.cloned.1.call-done = bf16[384,160]{1,0:T(8,128)(2,1)} async-done(((bf16[1536,160]{1,0:T(8,128)(2,1)}), bf16[384,160]{1,0:T(8,128)(2,1)}) %reduce-scatter.4.cloned.1.call-update) | async-done | bytes 122896
  138.6 1.1 copy.36
  139.7 30.5 %all-reduce.2 = (f32[384,160]{0,1:T(8,128)S(1)}, f32[1]{0:T(128)}) all-reduce(bf16[384,160]{0,1:T(8,128)(2,1)S(1)} %copy.36, f32[1]{0:T(128)} %bitcast.7), channel_id=1, replica_groups=mesh['dp'=4,'lat'=4,'lon'=2] {'lat','lon'}, use_global_device_ids=true, to_apply=%region_8.9 | all-reduce | flops 61441 | bytes 368648 | tf_op jit(solution)/shard_map/psum | solution.py:103
  170.2 0.7 broadcast_multiply_fusion
  (58 shorter events, 3.3 us)
Async XLA Ops:
  7.2 102.4 %all-gather.3.cloned.1.call-start = ((), (), s32[]{:S(2)}) async-start(), calls=%async_computation.1 | async-start | bytes 5898240 | tf_op jit(solution)/shard_map/all_gather | solution.py:64
  7.9 130.7 %reduce-scatter.4.cloned.1.call-start = ((), (), s32[]{:S(2)}) async-start(), calls=%async_computation.2 | async-start | bytes 983040
  11.2 3.3 %copy-start.6 = (s32[8,8]{1,0:T(8,128)S(1)}, s32[8,8]{1,0:T(8,128)}, u32[]{:S(2)}) copy-start(s32[8,8]{1,0:T(8,128)} %param.9) | copy-start | bytes 772
  11.2 4.2 %copy-start.3 = (bf16[1,4,8,8,160]{4,3,2,1,0:T(8,128)(2,1)S(1)}, bf16[1,4,8,8,160]{4,3,2,1,0:T(8,128)(2,1)}, u32[]{:S(2)}) copy-start(bf16[1,4,8,8,160]{4,3,2,1,0:T(8,128)(2,1)} %param.8) | copy-start | bytes 245764
  11.3 6.1 %copy-start.7 = (bf16[384]{0:T(512)(128)(2,1)S(1)}, bf16[384]{0:T(512)(128)(2,1)}, u32[]{:S(2)}) copy-start(bf16[384]{0:T(512)(128)(2,1)} %param.12) | copy-start | bytes 2308
  11.3 21.0 %copy-start.4 = (bf16[384,160]{0,1:T(8,128)(2,1)S(1)}, bf16[384,160]{0,1:T(8,128)(2,1)}, u32[]{:S(2)}) copy-start(bf16[384,160]{0,1:T(8,128)(2,1)} %param.11) | copy-start | bytes 368644
  11.5 43.2 %collective-permute-start = (bf16[1,4,8,4,4608]{4,2,3,1,0:T(8,128)(2,1)S(1)}, bf16[1,4,8,4,4608]{4,2,3,1,0:T(8,128)(2,1)}, u32[]{:S(2)}, u32[]{:S(2)}) collective-permute-start(bf16[1,4,8,4,4608]{4,2,3,1,0:T(8,128)(2,1)S(1)} %copy.37), channel_id=1, source_target_pairs={{0,1},{1,0},{2,3},{3,2},{4,5},{5,4},{6,7},{7,6},{8,9},{9,8},{10,11... | collective-permute-start | bytes 3538952 | tf_op jit(solution)/shard_map/ppermute | solution.py:14
  15.1 43.7 %collective-permute-start.2 = (s32[8,4]{1,0:T(8,128)}, s32[8,4]{1,0:T(8,128)S(1)}, u32[]{:S(2)}, u32[]{:S(2)}) collective-permute-start(s32[8,4]{1,0:T(8,128)} %get-tuple-element.23), channel_id=1, source_target_pairs={{0,1},{1,0},{2,3},{3,2},{4,5},{5,4},{6,7},{7,6},{8,9},{9,8},{10,11... | collective-permute-start | bytes 392 | tf_op jit(solution)/shard_map/ppermute | solution.py:14
  15.5 57.5 %collective-permute-start.4 = (bf16[1,4,8,4,160]{4,3,2,1,0:T(4,128)(2,1)S(1)}, bf16[1,4,8,4,160]{4,3,2,1,0:T(4,128)(2,1)S(1)}, u32[]{:S(2)}, u32[]{:S(2)}) collective-permute-start(bf16[1,4,8,4,160]{4,3,2,1,0:T(4,128)(2,1)S(1)} %get-tuple-element.19), channel_id=1, source_target_pairs={{0,1},{1,0},{2,3},{3,2},{4,5},{5,4},{6,7},{7,6},{8,9},{9,8},{10,11... | collective-permute-start | bytes 122888 | tf_op jit(solution)/shard_map/ppermute | solution.py:14
  56.6 3.9 %copy-start.8 = (f32[5]{0:T(128)S(1)}, f32[5]{0:T(128)}, u32[]{:S(2)}) copy-start(f32[5]{0:T(128)} %param.13) | copy-start | bytes 64
  56.6 16.2 %copy-start.9 = (f32[8]{0:T(128)S(1)}, f32[8]{0:T(128)}, u32[]{:S(2)}) copy-start(f32[8]{0:T(128)} %fusion.27) | copy-start | bytes 100
  58.8 18.8 %collective-permute-start.1 = (bf16[1,4,4,8,4608]{4,3,2,1,0:T(8,128)(2,1)}, bf16[1,4,4,8,4608]{4,3,2,1,0:T(8,128)(2,1)S(1)}, u32[]{:S(2)}, u32[]{:S(2)}) collective-permute-start(bf16[1,4,4,8,4608]{4,3,2,1,0:T(8,128)(2,1)} %get-tuple-element.11), channel_id=1, source_target_pairs={{0,6},{2,0},{4,2},{6,4},{1,7},{3,1},{5,3},{7,5},{8,14},{10,8},{12,... | collective-permute-start | bytes 3538952 | tf_op jit(solution)/shard_map/ppermute | solution.py:14
  58.9 14.0 %collective-permute-start.3 = (s32[4,8]{1,0:T(4,128)S(1)}, s32[4,8]{1,0:T(4,128)S(1)}, u32[]{:S(2)}, u32[]{:S(2)}) collective-permute-start(s32[4,8]{1,0:T(4,128)S(1)} %get-tuple-element.21), channel_id=1, source_target_pairs={{0,6},{2,0},{4,2},{6,4},{1,7},{3,1},{5,3},{7,5},{8,14},{10,8},{12,... | collective-permute-start | bytes 392 | tf_op jit(solution)/shard_map/ppermute | solution.py:14
  73.1 4.4 %collective-permute-start.5 = (bf16[1,4,4,8,160]{4,3,2,1,0:T(8,128)(2,1)S(1)}, bf16[1,4,4,8,160]{4,3,2,1,0:T(8,128)(2,1)S(1)}, u32[]{:S(2)}, u32[]{:S(2)}) collective-permute-start(bf16[1,4,4,8,160]{4,3,2,1,0:T(8,128)(2,1)S(1)} %get-tuple-element.17), channel_id=1, source_target_pairs={{0,6},{2,0},{4,2},{6,4},{1,7},{3,1},{5,3},{7,5},{8,14},{10,8},{12,... | collective-permute-start | bytes 122888 | tf_op jit(solution)/shard_map/ppermute | solution.py:14
  79.2 2.3 %copy-start = (bf16[2,128,1536]{1,2,0:T(8,128)(2,1)S(1)}, bf16[2,128,1536]{1,2,0:T(8,128)(2,1)}, u32[]{:S(2)}) copy-start(bf16[2,128,1536]{1,2,0:T(8,128)(2,1)} %copy.29) | copy-start | bytes 2359300
  79.2 2.3 %copy-start.5 = (pred[128,128]{0,1:T(8,128)(4,1)S(1)}, pred[128,128]{0,1:T(8,128)(4,1)}, u32[]{:S(2)}) copy-start(pred[128,128]{0,1:T(8,128)(4,1)} %broadcast_compare_fusion) | copy-start | bytes 49156
  80.4 1.2 copy-start.1
  81.6 4.2 %copy-start.2 = (bf16[2,128,1536]{1,2,0:T(8,128)(2,1)S(1)}, bf16[2,128,1536]{1,2,0:T(8,128)(2,1)}, u32[]{:S(2)}) copy-start(bf16[2,128,1536]{1,2,0:T(8,128)(2,1)} %copy.28) | copy-start | bytes 2359300
Sparse Core Ops, SparseCore 0:
  9.6 99.9 all-gather.2
  116.8 21.7 reduce-scatter.3
where the time goes:
time: 178 us
  blocking collectives  65.2 us (37%)
  waiting for transfers between devices  50 us (28%)
  matrix products  17.8 us (10%)
  between operations  15.6 us (9%)
  local copies, waits for them, and re-layouts  13.3 us (7%)
  starting transfers between devices  9.26 us (5%)
  other arithmetic  6.65 us (4%)
    psum x1, blocking collectives, shards(): grad_sum, loss_sum = lax.psum((grad_shard, shard_penalty), ('lat', 'lon'))  30.5 us
    all_gather x1, blocking collectives, shards(): lax.all_gather(unpatch_matrix, 'dp', axis=0, tiled=True)  21.7 us
    all_gather x1, waiting for transfers between devices, shards(): lax.all_gather(w_out, 'dp', axis=0, tiled=True)  19.3 us
    unnamed x3, waiting for transfers between devices  16.6 us
    ppermute x6, waiting for transfers between devices, from_behind(): lax.ppermute(array, axis, [(i, (i + by) % length) for i in range(length)])  14.1 us
    all_gather x1, blocking collectives, shards(): lax.all_gather(norm_gain, 'dp', axis=0, tiled=True)  13 us
    ppermute x6, starting transfers between devices, from_behind(): lax.ppermute(array, axis, [(i, (i + by) % length) for i in range(length)])  9.19 us
    dot_general x1, matrix products, shards(): jnp.einsum('tj,ij->ti', grad_mixed, out_all, preferred_element_type=jnp.f...  4.79 us
  transfers between devices with their start and end apart: 8, of which 4 were waited for; matrix products, arithmetic and copies ran while one was open for 16% of the time, Pallas kernels for 0%

commit v1 on v0

--- a/solution.py
+++ b/solution.py
@@ -7,6 +7,28 @@
 HEADS = 48
 HDIM = 32
 WLEV = 2
+
+
+def laid_out(blocks, dim):
+    blocks = jnp.moveaxis(blocks, 0, dim)
+    shape = blocks.shape
+    return blocks.reshape(*shape[:dim], shape[dim] * shape[dim + 1], *shape[dim + 2 :])
+
+
+def gather_around(x, axis, dim):
+    count = lax.axis_size(axis)
+    pairs = [(i, (i + 1) % count) for i in range(count)]
+    back = [(b, a) for a, b in pairs]
+    lower, upper = ([], [])
+    for hop in range(count - 1):
+        if hop % 2 == 0:
+            lower.append(lax.ppermute(lower[-1] if lower else x, axis, pairs))
+        else:
+            upper.append(lax.ppermute(upper[-1] if upper else x, axis, back))
+    tiles = jnp.stack([*lower[::-1], x, *upper])
+    shift = lax.axis_index(axis) - len(lower)
+    tiles = tiles[(jnp.arange(count) - shift) % count]
+    return laid_out(tiles, dim)
 
 
 def from_behind(array, axis, by):
@@ -61,7 +83,7 @@
     context = context.astype(jnp.bfloat16).reshape(win_count * tokw, model_width)
     element_total = win_count * tokw
     out_all, unprojected_pieces, gain_all = (
-        lax.all_gather(w_out, "dp", axis=0, tiled=True),
+        gather_around(w_out, "dp", 0),
         lax.all_gather(unpatch_matrix, "dp", axis=0, tiled=True),
         lax.all_gather(norm_gain, "dp", axis=0, tiled=True),
     )

time: 178 us -> 217 us (1.22)
  blocking collectives: 65.2 us -> 95.3 us
  local copies, waits for them, and re-layouts: 13.3 us -> 18.1 us
  starting transfers between devices: 9.26 us -> 13 us
  other arithmetic: 6.65 us -> 9.36 us
  waiting for transfers between devices: 50 us -> 47.5 us
    all_gather x1, blocking collectives: 13 us -> 49.6 us  [shards(): lax.all_gather(norm_gain, 'dp', axis=0, tiled=True)]
    all_gather x1 -> x0, waiting for transfers between devices: 19.3 us -> none  [shards(): lax.all_gather(w_out, 'dp', axis=0, tiled=True)]
    ppermute x0 -> x3, waiting for transfers between devices: none -> 17.4 us  [the longest x2 17.4 us: gather_around(): lower.append(lax.ppermute(lower[-1] if lower else x, axis, pairs))]
    all_gather x1, blocking collectives: 21.7 us -> 15.2 us  [shards(): lax.all_gather(unpatch_matrix, 'dp', axis=0, tiled=True)]
    ppermute x0 -> x3, starting transfers between devices: none -> 5.67 us  [the longest x2 3.58 us: gather_around(): lower.append(lax.ppermute(lower[-1] if lower else x, axis, pairs))]
    gather x0 -> x1, local copies, waits for them, and re-layouts: none -> 5.34 us  [gather_around(): tiles = tiles[(jnp.arange(count) - shift) % count]]
    another operation x0 -> x1, other arithmetic: none -> 3.82 us  [gather_around(): tiles = jnp.stack([*lower[::-1], x, *upper])]
    unnamed x3 -> x2, waiting for transfers between devices: 16.6 us -> 16 us
  transfers between devices with their start and end apart: 8 -> 10, of which waited for: 4 -> 4; matrix products, arithmetic and copies ran while one was open for 16% -> 13% of each run, Pallas kernels for 0% -> 0%
where the time goes in v1:
time: 217 us
  blocking collectives  95.3 us (44%)
  waiting for transfers between devices  47.5 us (22%)
  local copies, waits for them, and re-layouts  18.1 us (8%)
  matrix products  17.8 us (8%)
  between operations  15.6 us (7%)
  starting transfers between devices  13 us (6%)
  other arithmetic  9.36 us (4%)
    all_gather x1, blocking collectives, shards(): lax.all_gather(norm_gain, 'dp', axis=0, tiled=True)  49.6 us
    psum x1, blocking collectives, shards(): grad_sum, loss_sum = lax.psum((grad_shard, shard_penalty), ('lat', 'lon'))  30.4 us
    ppermute x2, waiting for transfers between devices, gather_around(): lower.append(lax.ppermute(lower[-1] if lower else x, axis, pairs))  17.4 us
    unnamed x2, waiting for transfers between devices  16 us
    all_gather x1, blocking collectives, shards(): lax.all_gather(unpatch_matrix, 'dp', axis=0, tiled=True)  15.2 us
    ppermute x6, waiting for transfers between devices, from_behind(): lax.ppermute(array, axis, [(i, (i + by) % length) for i in range(length)])  14.1 us
    ppermute x6, starting transfers between devices, from_behind(): lax.ppermute(array, axis, [(i, (i + by) % length) for i in range(length)])  7.31 us
    gather x1, local copies, waits for them, and re-layouts, gather_around(): tiles = tiles[(jnp.arange(count) - shift) % count]  5.34 us
  transfers between devices with their start and end apart: 10, of which 4 were waited for; matrix products, arithmetic and copies ran while one was open for 13% of the time, Pallas kernels for 0%

profile of v1, /device:TPU:0, one launch (start us, length us, event | category | flops | bytes accessed | tf_op | source)
XLA Modules:
  0.0 216.6 jit_solution(4051264161345421161)
XLA Ops:
  7.2 3.1 %collective-permute-start.2 = (bf16[384,1536]{1,0:T(8,128)(2,1)}, bf16[384,1536]{1,0:T(8,128)(2,1)}, u32[]{:S(2)}, u32[]{:S(2)}) collective-permute-start(bf16[384,1536]{1,0:T(8,128)(2,1)} %param.10), channel_id=1, source_target_pairs={{0,8},{8,16},{16,24},{24,0},{1,9},{9,17},{17,25},{25,1},{2,10},{10... | collective-permute-start | bytes 3538952 | tf_op jit(solution)/shard_map/ppermute | solution.py:25
  10.3 2.1 collective-permute-start.4
  12.4 3.3 %fusion.35 = (bf16[1,4,8,4,4608]{4,3,2,1,0:T(4,128)(2,1)S(1)}, bf16[1,4,8,4,4608]{4,3,2,1,0:T(4,128)(2,1)S(1)}) fusion(bf16[1,4,8,8,4608]{4,3,2,1,0:T(8,128)(2,1)} %param.7), kind=kLoop, calls=%fused_computation.79 | loop fusion | bytes 4718592 | tf_op jit(solution)/shard_map/slice | solution.py:53
  15.9 1.7 collective-permute-start
  18.1 1.7 collective-permute-start.7
  20.0 49.6 %all-gather = bf16[4,1,384]{2,1,0:T(2,128)(2,1)S(1)} all-gather(bf16[1,1,384]{2,1,0:T(2,128)(2,1)S(1)} %reshape.226), channel_id=1, replica_groups=mesh['dp'=4,'lat'=4,'lon'=2] {'dp'}, dimensions={0}, use_global_device_ids=true | all-gather | bytes 3840 | tf_op jit(solution)/shard_map/all_gather | solution.py:88
  69.7 0.6 cosine_reduce_fusion
  71.1 15.2 %all_gather.7 = bf16[1536,160]{0,1:T(8,128)(2,1)S(1)} all-gather(bf16[384,160]{0,1:T(8,128)(2,1)S(1)} %copy-done.5), channel_id=1, replica_groups=mesh['dp'=4,'lat'=4,'lon'=2] {'dp'}, dimensions={0}, use_global_device_ids=true | all-gather | bytes 614400 | tf_op jit(solution)/shard_map/all_gather | solution.py:87
  86.4 1.9 copy.27
  88.3 2.1 fusion.8
  90.6 1.6 collective-permute-start.6
  92.4 12.2 %collective-permute-done.6 = s32[4,8]{1,0:T(4,128)S(1)} collective-permute-done((s32[4,8]{1,0:T(4,128)S(1)}, s32[4,8]{1,0:T(4,128)S(1)}, u32[]{:S(2)}, u32[]{:S(2)}) %collective-permute-start.6) | collective-permute-done | bytes 160 | tf_op jit(solution)/shard_map/ppermute | solution.py:36
  104.8 1.9 collective-permute-start.8
  106.7 1.9 collective-permute-done.8
  109.7 1.2 copy.29
  110.8 1.2 copy.30
  112.0 1.2 copy.28
  113.2 4.2 %fusion.39 = (f32[2,48,128]{2,1,0:T(8,128)S(1)}, f32[2,48,128,128]{2,3,1,0:T(8,128)}) fusion(pred[128,128]{0,1:T(8,128)(4,1)S(1)} %broadcast_compare_fusion, bf16[2,128,48,32]{1,3,2,0:T(8,128)(2,1)S(1)} %bitcast.46, bf16[2,128,48,32]{1,3,2,0:T(8,128)(2,1)S(1)} %bitcast.47), kind=kOutput, calls=%fused_computation.83 | convolution fusion | flops 106954880 | bytes 7929856 | tf_op jit(solution)/shard_map/sub | solution.py:80
  117.3 3.7 %fusion.7 = bf16[2,128,48,32]{1,3,2,0:T(8,128)(2,1)S(1)} fusion(bf16[2,128,48,32]{1,3,2,0:T(8,128)(2,1)S(1)} %bitcast.48, f32[2,48,128,128]{2,3,1,0:T(8,128)} %get-tuple-element.25, f32[2,48,128]{2,1,0:T(8,128)S(1)} %get-tuple-element.24), kind=kOutput, calls=%fused_computation.23 | convolution fusion | flops 104202240 | bytes 7913472 | tf_op jit(solution)/shard_map/whqk,wkhd->wqhd/dot_general | solution.py:82
  121.0 0.8 copy.32
  121.9 17.4 %collective-permute-done.3 = bf16[384,1536]{1,0:T(8,128)(2,1)} collective-permute-done((bf16[384,1536]{1,0:T(8,128)(2,1)}, bf16[384,1536]{1,0:T(8,128)(2,1)}, u32[]{:S(2)}, u32[]{:S(2)}) %collective-permute-start.3) | collective-permute-done | bytes 1179680 | tf_op jit(solution)/shard_map/ppermute | solution.py:25
  139.3 3.8 %pad_maximum_fusion = bf16[4,384,1536]{2,1,0:T(8,128)(2,1)} fusion(bf16[1,384,1536]{2,1,0:T(8,128)(2,1)} %bitcast.8, bf16[1,384,1536]{2,1,0:T(8,128)(2,1)S(1)} %bitcast.44, bf16[1,384,1536]{2,1,0:T(8,128)(2,1)} %bitcast.6, bf16[1,384,1536]{2,1,0:T(8,128)(2,1)} %bitcast.5), kind=kLoop, calls=%fused_computation.6 | loop fusion | flops 7077888 | bytes 9437184 | tf_op jit(solution)/shard_map/stack | solution.py:28
  143.1 5.3 %gather_fusion = bf16[4,384,1536]{2,1,0:T(8,128)(2,1)} fusion(bf16[4,384,1536]{2,1,0:T(8,128)(2,1)} %pad_maximum_fusion, s32[1024]{0:T(1024)S(1)} %pad_clamp_fusion), kind=kCustom, calls=%fused_computation | custom fusion | bytes 9437200 | tf_op jit(solution)/shard_map/gather | solution.py:30
  148.4 3.8 %fusion.40 = (f32[256]{0:T(256)S(1)}, f32[256,1536]{1,0:T(8,128)S(1)}) fusion(bf16[1536,1536]{1,0:T(8,128)(2,1)} %bitcast.42, bf16[192,8,2,128]{3,2,1,0:T(2,128)(2,1)S(1)} %bitcast.45), kind=kOutput, calls=%fused_computation.84 | convolution fusion | flops 1208352512 | bytes 7078912 | tf_op jit(solution)/shard_map/dot_general | solution.py:90
  153.3 0.7 fusion.18
  154.3 1.2 copy.35
  156.1 0.6 fusion.33
  156.8 4.8 %convolution_convert_fusion = bf16[256,1536]{1,0:T(8,128)(2,1)} fusion(bf16[1536,1536]{1,0:T(8,128)(2,1)} %bitcast.43, f32[256,1536]{1,0:T(8,128)S(1)} %get-tuple-element.28, f32[256,1536]{1,0:T(8,128)S(1)} %get-tuple-element.27, f32[256]{0:T(256)S(1)} %get-tuple-element.29, f32[256]{0:T(256)S(1)} %get-tuple-element.30, f32[256]{0:T(256)S(1)} %add_rsqrt_fusion, ...), kind=kOutput, calls=%fused_computation.12 | convolution fusion | flops 1211105280 | bytes 8654848 | tf_op jit(solution)/shard_map/tj,ij->ti/dot_general | solution.py:137
  161.6 16.0 %reduce-scatter.4.cloned.1.call-done = bf16[384,160]{1,0:T(8,128)(2,1)} async-done(((bf16[1536,160]{1,0:T(8,128)(2,1)}), bf16[384,160]{1,0:T(8,128)(2,1)}) %reduce-scatter.4.cloned.1.call-update) | async-done | bytes 122896
  177.5 1.1 copy.36
  178.6 30.4 %all-reduce.2 = (f32[384,160]{0,1:T(8,128)S(1)}, f32[1]{0:T(128)}) all-reduce(bf16[384,160]{0,1:T(8,128)(2,1)S(1)} %copy.36, f32[1]{0:T(128)} %bitcast.13), channel_id=1, replica_groups=mesh['dp'=4,'lat'=4,'lon'=2] {'lat','lon'}, use_global_device_ids=true, to_apply=%region_8.9 | all-reduce | flops 61441 | bytes 368648 | tf_op jit(solution)/shard_map/psum | solution.py:125
  209.0 0.7 broadcast_multiply_fusion
  (63 shorter events, 4.1 us)
Async XLA Ops:
  7.2 170.4 %reduce-scatter.4.cloned.1.call-start = ((), (), s32[]{:S(2)}) async-start(), calls=%async_computation.1 | async-start | bytes 983040
  7.2 101.5 %collective-permute-start.2 = (bf16[384,1536]{1,0:T(8,128)(2,1)}, bf16[384,1536]{1,0:T(8,128)(2,1)}, u32[]{:S(2)}, u32[]{:S(2)}) collective-permute-start(bf16[384,1536]{1,0:T(8,128)(2,1)} %param.10), channel_id=1, source_target_pairs={{0,8},{8,16},{16,24},{24,0},{1,9},{9,17},{17,25},{25,1},{2,10},{10... | collective-permute-start | bytes 3538952 | tf_op jit(solution)/shard_map/ppermute | solution.py:25
  10.3 111.6 %collective-permute-start.4 = (bf16[384,1536]{1,0:T(8,128)(2,1)}, bf16[384,1536]{1,0:T(8,128)(2,1)}, u32[]{:S(2)}, u32[]{:S(2)}) collective-permute-start(bf16[384,1536]{1,0:T(8,128)(2,1)} %param.10), channel_id=1, source_target_pairs={{8,0},{16,8},{24,16},{0,24},{9,1},{17,9},{25,17},{1,25},{10,2},{18... | collective-permute-start | bytes 3538952 | tf_op jit(solution)/shard_map/ppermute | solution.py:27
  15.7 2.0 copy-start.6
  15.7 2.4 %copy-start.4 = (bf16[1,4,8,8,160]{4,3,2,1,0:T(8,128)(2,1)S(1)}, bf16[1,4,8,8,160]{4,3,2,1,0:T(8,128)(2,1)}, u32[]{:S(2)}) copy-start(bf16[1,4,8,8,160]{4,3,2,1,0:T(8,128)(2,1)} %param.8) | copy-start | bytes 245764
  15.7 4.3 %copy-start.7 = (bf16[384]{0:T(512)(128)(2,1)S(1)}, bf16[384]{0:T(512)(128)(2,1)}, u32[]{:S(2)}) copy-start(bf16[384]{0:T(512)(128)(2,1)} %param.12) | copy-start | bytes 2308
  15.7 55.4 %copy-start.5 = (bf16[384,160]{0,1:T(8,128)(2,1)S(1)}, bf16[384,160]{0,1:T(8,128)(2,1)}, u32[]{:S(2)}) copy-start(bf16[384,160]{0,1:T(8,128)(2,1)} %param.11) | copy-start | bytes 368644
  15.9 70.5 %collective-permute-start = (bf16[1,4,8,4,4608]{4,2,3,1,0:T(8,128)(2,1)S(1)}, bf16[1,4,8,4,4608]{4,2,3,1,0:T(8,128)(2,1)}, u32[]{:S(2)}, u32[]{:S(2)}) collective-permute-start(bf16[1,4,8,4,4608]{4,2,3,1,0:T(8,128)(2,1)S(1)} %copy.37), channel_id=1, source_target_pairs={{0,1},{1,0},{2,3},{3,2},{4,5},{5,4},{6,7},{7,6},{8,9},{9,8},{10,11... | collective-permute-start | bytes 3538952 | tf_op jit(solution)/shard_map/ppermute | solution.py:36
  17.7 72.8 %collective-permute-start.5 = (s32[8,4]{1,0:T(8,128)S(1)}, s32[8,4]{1,0:T(8,128)S(1)}, u32[]{:S(2)}, u32[]{:S(2)}) collective-permute-start(s32[8,4]{1,0:T(8,128)S(1)} %get-tuple-element.23), channel_id=1, source_target_pairs={{0,1},{1,0},{2,3},{3,2},{4,5},{5,4},{6,7},{7,6},{8,9},{9,8},{10,11... | collective-permute-start | bytes 392 | tf_op jit(solution)/shard_map/ppermute | solution.py:36
  18.1 86.5 %collective-permute-start.7 = (bf16[1,4,8,4,160]{4,3,2,1,0:T(4,128)(2,1)S(1)}, bf16[1,4,8,4,160]{4,3,2,1,0:T(4,128)(2,1)S(1)}, u32[]{:S(2)}, u32[]{:S(2)}) collective-permute-start(bf16[1,4,8,4,160]{4,3,2,1,0:T(4,128)(2,1)S(1)} %get-tuple-element.19), channel_id=1, source_target_pairs={{0,1},{1,0},{2,3},{3,2},{4,5},{5,4},{6,7},{7,6},{8,9},{9,8},{10,11... | collective-permute-start | bytes 122888 | tf_op jit(solution)/shard_map/ppermute | solution.py:36
  88.3 3.9 %copy-start.8 = (f32[5]{0:T(128)S(1)}, f32[5]{0:T(128)}, u32[]{:S(2)}) copy-start(f32[5]{0:T(128)} %param.13) | copy-start | bytes 64
  90.5 18.8 %collective-permute-start.1 = (bf16[1,4,4,8,4608]{4,3,2,1,0:T(8,128)(2,1)}, bf16[1,4,4,8,4608]{4,3,2,1,0:T(8,128)(2,1)S(1)}, u32[]{:S(2)}, u32[]{:S(2)}) collective-permute-start(bf16[1,4,4,8,4608]{4,3,2,1,0:T(8,128)(2,1)} %get-tuple-element.11), channel_id=1, source_target_pairs={{0,6},{2,0},{4,2},{6,4},{1,7},{3,1},{5,3},{7,5},{8,14},{10,8},{12,... | collective-permute-start | bytes 3538952 | tf_op jit(solution)/shard_map/ppermute | solution.py:36
  90.6 14.0 %collective-permute-start.6 = (s32[4,8]{1,0:T(4,128)S(1)}, s32[4,8]{1,0:T(4,128)S(1)}, u32[]{:S(2)}, u32[]{:S(2)}) collective-permute-start(s32[4,8]{1,0:T(4,128)S(1)} %get-tuple-element.21), channel_id=1, source_target_pairs={{0,6},{2,0},{4,2},{6,4},{1,7},{3,1},{5,3},{7,5},{8,14},{10,8},{12,... | collective-permute-start | bytes 392 | tf_op jit(solution)/shard_map/ppermute | solution.py:36
  104.8 3.8 %collective-permute-start.8 = (bf16[1,4,4,8,160]{4,3,2,1,0:T(8,128)(2,1)S(1)}, bf16[1,4,4,8,160]{4,3,2,1,0:T(8,128)(2,1)S(1)}, u32[]{:S(2)}, u32[]{:S(2)}) collective-permute-start(bf16[1,4,4,8,160]{4,3,2,1,0:T(8,128)(2,1)S(1)} %get-tuple-element.17), channel_id=1, source_target_pairs={{0,6},{2,0},{4,2},{6,4},{1,7},{3,1},{5,3},{7,5},{8,14},{10,8},{12,... | collective-permute-start | bytes 122888 | tf_op jit(solution)/shard_map/ppermute | solution.py:36
  108.8 30.5 %collective-permute-start.3 = (bf16[384,1536]{1,0:T(8,128)(2,1)}, bf16[384,1536]{1,0:T(8,128)(2,1)}, u32[]{:S(2)}, u32[]{:S(2)}) collective-permute-start(bf16[384,1536]{1,0:T(8,128)(2,1)} %collective-permute-done.2), channel_id=1, source_target_pairs={{0,8},{8,16},{16,24},{24,0},{1,9},{9,17},{17,25},{25,1},{2,10},{10... | collective-permute-start | bytes 3538952 | tf_op jit(solution)/shard_map/ppermute | solution.py:25
  110.8 2.3 %copy-start.1 = (bf16[2,128,1536]{1,2,0:T(8,128)(2,1)S(1)}, bf16[2,128,1536]{1,2,0:T(8,128)(2,1)}, u32[]{:S(2)}) copy-start(bf16[2,128,1536]{1,2,0:T(8,128)(2,1)} %copy.29) | copy-start | bytes 2359300
  112.0 1.2 copy-start.2
  113.2 4.2 %copy-start.3 = (bf16[2,128,1536]{1,2,0:T(8,128)(2,1)S(1)}, bf16[2,128,1536]{1,2,0:T(8,128)(2,1)}, u32[]{:S(2)}) copy-start(bf16[2,128,1536]{1,2,0:T(8,128)(2,1)} %copy.28) | copy-start | bytes 2359300
  121.0 18.2 %copy-start = (bf16[384,1536]{1,0:T(8,128)(2,1)S(1)}, bf16[384,1536]{1,0:T(8,128)(2,1)}, u32[]{:S(2)}) copy-start(bf16[384,1536]{1,0:T(8,128)(2,1)} %param.10) | copy-start | bytes 3538948
Sparse Core Ops, SparseCore 0:
  155.6 21.8 reduce-scatter.3
